TPU v7x, 32 devices: a whole 2x2x4 slice. The times are simulated.
32 devices in a mesh: lat: 8 (over z, core), lon: 4 (over y, x).
Axes of the slice: x: 2, y: 2, z: 4, core: 2. Of those that a mesh axis runs over, the one named last changes fastest.
Arguments:
- latent: float32 [64, 112, 640], P('lat', 'lon'), may hold values from -6 to 6
- conv_first: float32 [25, 640], replicated, may hold values from -1.2 to 1.2
- conv_second: float32 [25, 640], replicated, may hold values from -1.2 to 1.2
- filter_gains: float32 [48, 640], P(None, 'lon'), may hold values from -4 to 4
- norm_gain: float32 [640], replicated, may hold values from 0.5 to 1.5
- up_weight: bfloat16 [640, 1280], replicated, may hold values from -0.25 to 0.25
- down_weight: bfloat16 [1280, 640], replicated, may hold values from -0.15625 to 0.15625
Outputs:
- block_out: float32 [64, 112, 640], P('lat', 'lon')
All inputs are finite; a program needn't handle non-finite values.
Results may differ from a plain program's by a relative error of at most 0.0012.
Values sent between devices are 32-bit elements; how exact they have to be, the bound alone decides.
A program may use at most 64 MiB of HBM per device.

v0:
```python
import jax
import jax.numpy as jnp
from jax import lax
from jax.sharding import PartitionSpec as P

highest = lax.Precision.HIGHEST


def padded_2(block, sides, width):
    for axis, dim in sides:
        count = lax.axis_size(axis)
        forward = [(i, i + 1) for i in range(count - 1)]
        backward = [(target, source) for source, target in forward]
        low = lax.ppermute(
            lax.slice_in_dim(block, block.shape[dim] - width, None, axis=dim), axis, forward
        )
        high = lax.ppermute(lax.slice_in_dim(block, 0, width, axis=dim), axis, backward)
        block = jnp.concatenate([low, block, high], axis=dim)
    return block


def stencil_sum(padded, weights, row_count, col_count):
    stencil_total = jnp.zeros((row_count, col_count, padded.shape[2]), padded.dtype)
    for row_shift in range(5):
        for col_shift in range(5):
            stencil_total = (
                stencil_total
                + weights[row_shift * 5 + col_shift]
                * padded[row_shift : row_shift + row_count, col_shift : col_shift + col_count, :]
            )
    return stencil_total


def slice_stencil(sliced, weights):
    lat_extended = padded_2(sliced, (("lat", 0),), 2)
    wrapped = jnp.concatenate([lat_extended[:, -2:], lat_extended, lat_extended[:, :2]], axis=1)
    return stencil_sum(wrapped, weights, sliced.shape[0], sliced.shape[1])


def colatitude(cell_count, float_type):
    cell_index = jnp.arange(cell_count).astype(float_type)
    return jnp.pi * (cell_index + 0.5) / cell_count


def legendre_table(orders, degrees, cosine, sine_theta):
    log_seed = 0.5 * (
        jnp.log((2.0 * orders + 1.0) / (4.0 * jnp.pi))
        + jax.scipy.special.gammaln(2.0 * orders + 1.0)
        - 2.0 * orders * jnp.log(2.0)
        - 2.0 * jax.scipy.special.gammaln(orders + 1.0)
    )
    diagonal_term = jnp.exp(log_seed[:, None] + orders[:, None] * jnp.log(sine_theta)[None, :])
    blanks = jnp.zeros_like(diagonal_term)
    legendre = jnp.zeros((orders.shape[0], degrees, sine_theta.shape[0]), diagonal_term.dtype)

    def block_step(block_index, state_tuple):
        previous, earlier, legendre = state_tuple
        values = []
        for offset in range(8):
            degree = (block_index * 8 + offset).astype(diagonal_term.dtype)
            square = degree * degree
            upper_ratio = jnp.sqrt(
                jnp.maximum(4.0 * square - 1.0, 1.0) / jnp.maximum(square - orders * orders, 1.0)
            )
            below_sq = (degree - 1.0) * (degree - 1.0)
            lower_ratio = jnp.sqrt(
                jnp.maximum(below_sq - orders * orders, 0.0)
                / jnp.maximum(4.0 * below_sq - 1.0, 1.0)
            )
            recurred = upper_ratio[:, None] * (
                cosine[None, :] * previous - lower_ratio[:, None] * earlier
            )
            current = jnp.where(
                (degree < orders)[:, None],
                blanks,
                jnp.where((degree == orders)[:, None], diagonal_term, recurred),
            )
            values.append(current)
            earlier = previous
            previous = current
        stacked = jnp.stack(values, axis=1)
        legendre = lax.dynamic_update_slice(
            legendre, stacked, (jnp.int32(0), (block_index * 8).astype(jnp.int32), jnp.int32(0))
        )
        return (previous, earlier, legendre)

    return lax.fori_loop(0, degrees // 8, block_step, (blanks, blanks, legendre))[2]


def fourier_tables(lon_count, mode_count, float_type):
    product_index = jnp.arange(lon_count)[:, None] * jnp.arange(mode_count)[None, :] % lon_count
    phase_grid = 2.0 * jnp.pi * product_index.astype(float_type) / lon_count
    forward = jnp.stack([jnp.cos(phase_grid), -jnp.sin(phase_grid)], axis=1) / lon_count
    factor = jnp.where(jnp.arange(mode_count) == 0, 1.0, 2.0).astype(float_type)
    inverse = jnp.stack(
        [jnp.cos(phase_grid).T * factor[:, None], -jnp.sin(phase_grid).T * factor[:, None]], axis=0
    )
    return (forward, inverse)


def channel_mlp(latent, norm_gain, up_weight, down_weight):
    average = jnp.mean(latent, axis=-1, keepdims=True)
    centred = latent - average
    spread = jnp.mean(centred * centred, axis=-1, keepdims=True)
    normed = (centred * lax.rsqrt(spread + 1e-05) * norm_gain).astype(jnp.bfloat16)
    hidden = jnp.dot(normed, up_weight, preferred_element_type=jnp.float32)
    active = jax.nn.gelu(hidden, approximate=True).astype(jnp.bfloat16)
    return latent + jnp.dot(active, down_weight, preferred_element_type=jnp.float32)


def per_device(latent, conv_first, conv_second, filter_gains, norm_gain, up_weight, down_weight):
    lat_size = lax.axis_size("lat")
    lon_size = lax.axis_size("lon")
    lat_local = latent.shape[0]
    lon_local = latent.shape[1]
    slice_width = filter_gains.shape[1]
    mode_count = filter_gains.shape[0]
    lat_count = lat_local * lat_size
    lon_count = lon_local * lon_size
    order_count = mode_count // lat_size
    channel_start = lax.axis_index("lon") * slice_width
    sliced = lax.all_to_all(latent, "lon", split_axis=2, concat_axis=1, tiled=True)
    first_taps = lax.dynamic_slice_in_dim(conv_first, channel_start, slice_width, 1)
    first_sliced = sliced + slice_stencil(sliced, first_taps)
    forward, inverse = fourier_tables(lon_count, mode_count, jnp.float32)
    colat_grid = colatitude(lat_count, jnp.float32)
    orders = (lax.axis_index("lat") * order_count + jnp.arange(order_count)).astype(jnp.float32)
    legendre = legendre_table(orders, mode_count, jnp.cos(colat_grid), jnp.sin(colat_grid))
    quadrature = 2.0 * jnp.pi * jnp.pi * jnp.sin(colat_grid) / lat_count
    weighted = legendre * quadrature
    coeffs = jnp.einsum("inc,nrk->irkc", first_sliced, forward, precision=highest)
    spectrum = jnp.einsum(
        "kli,irkc->lrkc",
        weighted,
        lax.all_to_all(coeffs, "lat", split_axis=2, concat_axis=0, tiled=True),
        precision=highest,
    )
    spectrum = spectrum * filter_gains[:, None, None, :]
    restored = jnp.einsum("kli,lrkc->irkc", legendre, spectrum, precision=highest)
    returned = lax.all_to_all(restored, "lat", split_axis=0, concat_axis=2, tiled=True)
    filtered = jnp.einsum("irkc,rkn->inc", returned, inverse, precision=highest)
    second_taps = lax.dynamic_slice_in_dim(conv_second, channel_start, slice_width, 1)
    second_sliced = first_sliced + filtered
    incoming = second_sliced + slice_stencil(second_sliced, second_taps)
    arrived = lax.all_to_all(incoming, "lon", split_axis=1, concat_axis=2, tiled=True)
    return channel_mlp(arrived, norm_gain, up_weight, down_weight)


def solution(mesh):
    return jax.shard_map(
        per_device,
        mesh=mesh,
        in_specs=(P("lat", "lon", None), P(), P(), P(None, "lon"), P(), P(), P()),
        out_specs=P("lat", "lon", None),
        check_vma=False,
    )
```

profile of v0, /device:TPU:0, one launch (start us, length us, event | category | flops | bytes accessed | tf_op | source)
XLA Modules:
  0.0 142.4 jit_solution(8589328310714632998)
XLA Ops:
  0.0 3.1 %copy.101 = f32[8,28,640]{1,0,2:T(8,128)} copy(f32[8,28,640]{2,0,1:T(8,128)} %param.9) | data formatting | bytes 1146880 | tf_op args[0]
  3.1 4.9 %reshape.807 = f32[4,1,35840]{2,1,0:T(1,128)} reshape(f32[640,8,28]{2,1,0:T(8,128)} %bitcast.203) | data formatting | bytes 1146880
  8.1 5.2 %all-to-all-start = ((f32[4,1,35840]{2,1,0:T(1,128)}), f32[4,1,35840]{2,1,0:T(1,128)S(1)}, u32[]{:S(2)}, u32[]{:S(2)}) async-start(f32[4,1,35840]{2,1,0:T(1,128)} %reshape.807), calls=%async_computation | async-start | bytes 1146880 | tf_op jit(solution)/shard_map/all_to_all | solution.py:122
  13.3 1.8 %fusion.153 = (f32[1,160]{1,0:T(1,128)}, f32[1,160]{1,0:T(1,128)}, f32[1,160]{1,0:T(1,128)}, f32[1,160]{1,0:T(1,128)}, f32[1,160]{1,0:T(1,128)}, /*index=5*/f32[...) fusion(f32[25,640]{1,0:T(8,128)} %param.11, ...), kind=kLoop, calls=%fused_computation.298 | loop fusion | bytes 17952 | tf_op jit(solution)/shard_map/slice | solution.py:28
  15.2 2.0 %constant_dynamic-slice_fusion = (f32[1,160]{1,0:T(1,128)}, f32[1,160]{1,0:T(1,128)}, f32[1,160]{1,0:T(1,128)}, f32[1,160]{1,0:T(1,128)}, f32[1,160]{1,0:T(1,128...) fusion(f32[25,640]{1,0:T(8,128)} %param.10, ...), kind=kLoop, calls=%fused_computation.287 | loop fusion | bytes 23112 | tf_op jit(solution)/shard_map/slice | solution.py:28
  17.2 4.6 %all-to-all-done = f32[4,1,35840]{2,1,0:T(1,128)S(1)} async-done(((f32[4,1,35840]{2,1,0:T(1,128)}), f32[4,1,35840]{2,1,0:T(1,128)S(1)}, u32[]{:S(2)}, u32[]{:S(2)}) %all-to-all-start) | async-done | bytes 573472 | tf_op jit(solution)/shard_map/all_to_all | solution.py:122
  21.8 0.5 broadcast.1423
  22.3 2.3 %reduce.2 = f32[4,35840]{1,0:T(4,128)S(1)} reduce(f32[4,1,35840]{2,1,0:T(1,128)S(1)} %all-to-all-done, f32[]{:T(128)} %broadcast.1423), dimensions={1}, to_apply=%all_to_all.52.reduce_sub_computation | reduce | bytes 1146884 | tf_op jit(solution)/shard_map/all_to_all | solution.py:122
  24.6 4.7 %reshape.808 = f32[640,8,28]{2,1,0:T(8,128)} reshape(f32[4,35840]{1,0:T(4,128)S(1)} %reduce.2) | data formatting | bytes 1146880
  29.3 2.6 %copy.102 = f32[8,28,4,160]{3,0,1,2:T(8,128)S(1)} copy(f32[8,28,4,160]{1,0,3,2:T(8,128)} %bitcast.202) | data formatting | bytes 1146880 | tf_op jit(solution)/shard_map/all_to_all | solution.py:122
  31.9 0.1 fusion.151
  32.1 0.8 copy.104
  32.9 1.3 collective-permute-start.1
  34.2 0.8 copy.103
  35.0 3.2 %collective-permute-start = (f32[2,112,160]{1,2,0:T(8,128)}, f32[2,112,160]{1,2,0:T(8,128)S(1)}, u32[]{:S(2)}, u32[]{:S(2)}) collective-permute-start(f32[2,112,160]{1,2,0:T(8,128)} %copy.103), channel_id=1, source_target_pairs={{0,4},{4,8},{8,12},{12,16},{16,20},{20,24},{24,28},{1,5},{5,9},{9,... | collective-permute-start | bytes 430088 | tf_op jit(solution)/shard_map/ppermute | solution.py:14
  38.2 0.7 subtract_multiply_fusion
  38.9 0.8 sine_negate_fusion
  39.6 0.4 copy.109
  40.1 0.3 fusion.150
  40.7 0.6 maximum_maximum_fusion
  41.6 3.4 %fusion.87 = f32[8,112,160]{1,2,0:T(8,128)S(1)} fusion(f32[8,112,160]{1,2,0:T(8,128)S(1)} %copy.109, f32[2,112,160]{1,2,0:T(8,128)S(1)} %collective-permute-done.1, f32[2,112,160]{1,2,0:T(8,128)S(1)} %collective-permute-done, f32[12,114,160]{1,2,0:T(8,128)S(1)} %get-tuple-element.445, f32[12,114,160]{1,2,0:T(8,128)S(1)} %get-tuple-element.444, ...), kind=kLoop, calls=%fused_computation.145 | loop fusion | flops 7741440 | bytes 12918400 | tf_op jit(solution)/shard_map/add | solution.py:124
  45.0 1.4 convolution_bitcast_fusion.1
  46.4 1.4 copy.110
  47.7 7.3 %all-to-all-start.1 = ((f32[8,2,48,160]{3,0,1,2:T(8,128)}), f32[8,2,48,160]{3,0,1,2:T(8,128)}, u32[]{:S(2)}, u32[]{:S(2)}) async-start(f32[8,2,48,160]{3,0,1,2:T(8,128)} %copy.110), calls=%async_computation.1 | async-start | bytes 1572864 | tf_op jit(solution)/shard_map/all_to_all | solution.py:135
  55.1 7.2 %while.24 = (s32[]{:T(128)}, f32[6,64]{1,0:T(8,128)S(1)}, f32[6,64]{1,0:T(8,128)S(1)}, f32[6,48,64]{2,0,1:T(8,128)S(1)}, s32[]{:T(128)}, /*index=5*/f32[64]{0:T(...) while((s32[]{:T(128)}, f32[6,64]{1,0:T(8,128)S(1)}, ...), condition=%wide.region_1.2_spmd.clone.clone.clone.clone, body=%wide.region_0.1_spmd.clone.clone.clone.clone.sunk | while | flops 54669 | bytes 237349 | solution.py:87
  62.3 13.8 %all-to-all-done.1 = f32[8,2,48,160]{3,0,1,2:T(8,128)} async-done(((f32[8,2,48,160]{3,0,1,2:T(8,128)}), f32[8,2,48,160]{3,0,1,2:T(8,128)}, u32[]{:S(2)}, u32[]{:S(2)}) %all-to-all-start.1) | async-done | bytes 491552 | tf_op jit(solution)/shard_map/all_to_all | solution.py:135
  76.1 1.8 %fusion.43 = f32[48,2,6,160]{3,0,1,2:T(8,128)S(1)} fusion(f32[48,160]{1,0:T(8,128)S(1)} %copy-done.5, f32[6,48,64,1]{2,0,1,3:T(8,128)S(1)} %multiply_bitcast_fusion, f32[8,8,2,6,160]{4,1,2,3,0:T(8,128)} %bitcast.37), kind=kOutput, calls=%fused_computation.86 | convolution fusion | flops 70871040 | bytes 964608 | tf_op jit(solution)/shard_map/kli,irkc->lrkc/dot_general | solution.py:132
  77.9 0.8 convolution_bitcast_fusion
  78.8 1.5 %copy.116 = f32[64,2,6,160]{3,1,2,0:T(2,128)} copy(f32[64,2,6,160]{3,0,1,2:T(8,128)S(1)} %convolution_bitcast_fusion) | data formatting | bytes 983040 | tf_op jit(solution)/shard_map/kli,lrkc->irkc/transpose | solution.py:139
  80.3 4.2 %all-to-all-start.2 = ((f32[64,2,6,160]{3,1,2,0:T(2,128)}), f32[64,2,6,160]{3,1,2,0:T(2,128)}, u32[]{:S(2)}, u32[]{:S(2)}) async-start(f32[64,2,6,160]{3,1,2,0:T(2,128)} %copy.116), calls=%async_computation.2 | async-start | bytes 1572864 | tf_op jit(solution)/shard_map/all_to_all | solution.py:140
  84.6 20.8 %all-to-all-done.2 = f32[64,2,6,160]{3,1,2,0:T(2,128)} async-done(((f32[64,2,6,160]{3,1,2,0:T(2,128)}), f32[64,2,6,160]{3,1,2,0:T(2,128)}, u32[]{:S(2)}, u32[]{:S(2)}) %all-to-all-start.2) | async-done | bytes 491552 | tf_op jit(solution)/shard_map/all_to_all | solution.py:140
  105.4 1.3 copy.151
  106.8 1.6 %fusion.42 = f32[8,112,160]{1,2,0:T(8,128)S(1)} fusion(f32[8,112,160]{1,2,0:T(8,128)S(1)} %fusion.87, f32[8,2,48,160]{3,0,2,1:T(8,128)S(1)} %bitcast.206, f32[1,48,112]{2,1,0:T(8,128)S(1)} %get-tuple-element.503, f32[1,48,112]{2,1,0:T(8,128)S(1)} %get-tuple-element.502), kind=kOutput, calls=%fused_computation.84 | convolution fusion | flops 165304832 | bytes 1681408 | tf_op jit(solution)/shard_map/irkc,rkn->inc/dot_general | solution.py:141
  108.5 1.3 collective-permute-start.3
  109.8 3.3 %collective-permute-start.2 = (f32[2,112,160]{1,2,0:T(8,128)S(1)}, f32[2,112,160]{1,2,0:T(8,128)S(1)}, u32[]{:S(2)}, u32[]{:S(2)}) collective-permute-start(f32[2,112,160]{1,2,0:T(8,128)S(1)} %get-tuple-element.450), channel_id=1, source_target_pairs={{0,4},{4,8},{8,12},{12,16},{16,20},{20,24},{24,28},{1,5},{5,9},{9,... | collective-permute-start | bytes 430088 | tf_op jit(solution)/shard_map/ppermute | solution.py:14
  113.1 1.4 constant_dynamic-slice_fusion.1
  114.6 0.3 fusion.149
  115.0 0.6 maximum_maximum_fusion.1
  115.7 3.3 %fusion.59 = f32[8,112,160]{1,2,0:T(8,128)S(1)} fusion(f32[8,112,160]{1,2,0:T(8,128)S(1)} %fusion.42, f32[2,112,160]{1,2,0:T(8,128)S(1)} %collective-permute-done.3, f32[2,112,160]{1,2,0:T(8,128)S(1)} %collective-permute-done.2, f32[12,114,160]{1,2,0:T(8,128)S(1)} %get-tuple-element.441, f32[12,114,160]{1,2,0:T(8,128)S(1)} %get-tuple-element.440, ...), kind=kLoop, calls=%fused_computation.117 | loop fusion | flops 7741440 | bytes 12918400 | tf_op jit(solution)/shard_map/add | solution.py:144
  119.0 0.4 copy.120
  119.5 16.1 %all_to_all.72 = f32[8,112,160]{2,0,1:T(8,128)S(1)} all-to-all(f32[8,112,160]{2,0,1:T(8,128)S(1)} %copy.120), channel_id=1, replica_groups=mesh['lat'=8,'lon'=4] {'lon'}, dimensions={1} | all-to-all | bytes 1146880 | tf_op jit(solution)/shard_map/all_to_all | solution.py:145
  135.6 1.6 %copy.121 = f32[8,28,4,160]{3,2,0,1:T(4,128)} copy(f32[8,28,4,160]{3,0,1,2:T(8,128)S(1)} %bitcast.199) | data formatting | bytes 1146880 | tf_op jit(solution)/shard_map/all_to_all | solution.py:145
  137.3 1.7 %all_to_all.67 = f32[8,28,640]{2,0,1:T(8,128)S(1)} reshape(f32[8,28,4,160]{3,2,0,1:T(4,128)} %copy.121) | data formatting | bytes 1146880 | tf_op jit(solution)/shard_map/all_to_all | solution.py:145
  139.1 0.2 multiply_reduce_fusion
  139.3 0.1 multiply_convert_fusion
  139.5 0.8 fusion.39
  140.3 0.6 copy-done.1
  140.9 1.5 %fusion.44 = f32[8,28,640]{2,0,1:T(8,128)} fusion(f32[8,28,640]{2,0,1:T(8,128)S(1)} %all_to_all.67, bf16[1280,640]{1,0:T(8,128)(2,1)S(1)} %copy-done.1, bf16[8,28,1280]{2,1,0:T(8,128)(2,1)S(1)} %fusion.39), kind=kOutput, calls=%fused_computation.87 | convolution fusion | flops 367144960 | bytes 3358720 | tf_op jit(solution)/shard_map/dot_general | solution.py:108
  (253 shorter events, 6.6 us)
Async XLA Ops:
  0.0 139.5 %copy-start = (bf16[640,1280]{1,0:T(8,128)(2,1)S(1)}, bf16[640,1280]{1,0:T(8,128)(2,1)}, u32[]{:S(2)}) copy-start(bf16[640,1280]{1,0:T(8,128)(2,1)} %param.14) | copy-start | bytes 4915204
  8.1 13.7 %all-to-all-start = ((f32[4,1,35840]{2,1,0:T(1,128)}), f32[4,1,35840]{2,1,0:T(1,128)S(1)}, u32[]{:S(2)}, u32[]{:S(2)}) async-start(f32[4,1,35840]{2,1,0:T(1,128)} %reshape.807), calls=%async_computation | async-start | bytes 1146880 | tf_op jit(solution)/shard_map/all_to_all | solution.py:122
  32.9 7.1 %collective-permute-start.1 = (f32[2,112,160]{1,2,0:T(8,128)}, f32[2,112,160]{1,2,0:T(8,128)S(1)}, u32[]{:S(2)}, u32[]{:S(2)}) collective-permute-start(f32[2,112,160]{1,2,0:T(8,128)} %copy.104), channel_id=1, source_target_pairs={{4,0},{8,4},{12,8},{16,12},{20,16},{24,20},{28,24},{5,1},{9,5},{13... | collective-permute-start | bytes 430088 | tf_op jit(solution)/shard_map/ppermute | solution.py:17
  35.0 5.0 %collective-permute-start = (f32[2,112,160]{1,2,0:T(8,128)}, f32[2,112,160]{1,2,0:T(8,128)S(1)}, u32[]{:S(2)}, u32[]{:S(2)}) collective-permute-start(f32[2,112,160]{1,2,0:T(8,128)} %copy.103), channel_id=1, source_target_pairs={{0,4},{4,8},{8,12},{12,16},{16,20},{20,24},{24,28},{1,5},{5,9},{9,... | collective-permute-start | bytes 430088 | tf_op jit(solution)/shard_map/ppermute | solution.py:14
  40.5 0.8 copy-start.14
  40.5 0.8 copy-start.15
  40.5 0.8 copy-start.16
  40.5 0.8 copy-start.17
  40.5 0.8 copy-start.18
  40.5 0.8 copy-start.19
  40.5 0.8 copy-start.20
  40.5 0.8 copy-start.21
  40.6 0.8 copy-start.22
  40.6 0.8 copy-start.23
  40.6 0.8 copy-start.24
  40.6 0.8 copy-start.25
  40.6 0.8 copy-start.26
  40.6 0.8 copy-start.27
  40.6 0.8 copy-start.28
  40.6 0.8 copy-start.29
  40.6 0.8 copy-start.30
  40.6 0.8 copy-start.31
  40.7 0.8 copy-start.32
  40.7 0.8 copy-start.33
  40.7 0.8 copy-start.34
  40.7 0.8 copy-start.35
  40.7 0.8 copy-start.36
  40.7 0.8 copy-start.37
  40.7 0.8 copy-start.38
  41.6 3.4 %copy-start.3 = (f32[112,1,48]{0,2,1:T(8,128)S(1)}, f32[112,1,48]{0,2,1:T(8,128)}, u32[]{:S(2)}) copy-start(f32[112,1,48]{0,2,1:T(8,128)} %get-tuple-element.511) | copy-start | bytes 64516
  41.6 3.4 %copy-start.4 = (f32[112,1,48]{0,2,1:T(8,128)S(1)}, f32[112,1,48]{0,2,1:T(8,128)}, u32[]{:S(2)}) copy-start(f32[112,1,48]{0,2,1:T(8,128)} %get-tuple-element.512) | copy-start | bytes 64516
  46.4 8.7 %copy-start.2 = (f32[6]{0:T(128)S(1)}, f32[6]{0:T(128)}, u32[]{:S(2)}) copy-start(f32[6]{0:T(128)} %subtract_multiply_fusion) | copy-start | bytes 76
  47.7 28.3 %all-to-all-start.1 = ((f32[8,2,48,160]{3,0,1,2:T(8,128)}), f32[8,2,48,160]{3,0,1,2:T(8,128)}, u32[]{:S(2)}, u32[]{:S(2)}) async-start(f32[8,2,48,160]{3,0,1,2:T(8,128)} %copy.110), calls=%async_computation.1 | async-start | bytes 1572864 | tf_op jit(solution)/shard_map/all_to_all | solution.py:135
  55.1 21.0 %copy-start.5 = (f32[48,160]{1,0:T(8,128)S(1)}, f32[48,160]{1,0:T(8,128)}, u32[]{:S(2)}) copy-start(f32[48,160]{1,0:T(8,128)} %param.12) | copy-start | bytes 92164
  80.3 25.2 %all-to-all-start.2 = ((f32[64,2,6,160]{3,1,2,0:T(2,128)}), f32[64,2,6,160]{3,1,2,0:T(2,128)}, u32[]{:S(2)}, u32[]{:S(2)}) async-start(f32[64,2,6,160]{3,1,2,0:T(2,128)} %copy.116), calls=%async_computation.2 | async-start | bytes 1572864 | tf_op jit(solution)/shard_map/all_to_all | solution.py:140
  108.5 6.0 %collective-permute-start.3 = (f32[2,112,160]{1,2,0:T(8,128)S(1)}, f32[2,112,160]{1,2,0:T(8,128)S(1)}, u32[]{:S(2)}, u32[]{:S(2)}) collective-permute-start(f32[2,112,160]{1,2,0:T(8,128)S(1)} %get-tuple-element.451), channel_id=1, source_target_pairs={{4,0},{8,4},{12,8},{16,12},{20,16},{24,20},{28,24},{5,1},{9,5},{13... | collective-permute-start | bytes 430088 | tf_op jit(solution)/shard_map/ppermute | solution.py:17
  109.8 4.7 %collective-permute-start.2 = (f32[2,112,160]{1,2,0:T(8,128)S(1)}, f32[2,112,160]{1,2,0:T(8,128)S(1)}, u32[]{:S(2)}, u32[]{:S(2)}) collective-permute-start(f32[2,112,160]{1,2,0:T(8,128)S(1)} %get-tuple-element.450), channel_id=1, source_target_pairs={{0,4},{4,8},{8,12},{12,16},{16,20},{20,24},{24,28},{1,5},{5,9},{9,... | collective-permute-start | bytes 430088 | tf_op jit(solution)/shard_map/ppermute | solution.py:14
  114.9 0.7 copy-start.7
  114.9 0.7 copy-start.8
  115.0 0.7 copy-start.9
  115.0 0.7 copy-start.10
  115.0 0.7 copy-start.11
  115.0 0.7 copy-start.12
  115.0 0.7 copy-start.13
  137.3 2.0 %copy-start.6 = (f32[640]{0:T(1024)S(1)}, f32[640]{0:T(1024)}, u32[]{:S(2)}) copy-start(f32[640]{0:T(1024)} %param.13) | copy-start | bytes 7684
  139.5 1.4 %copy-start.1 = (bf16[1280,640]{1,0:T(8,128)(2,1)S(1)}, bf16[1280,640]{1,0:T(8,128)(2,1)}, u32[]{:S(2)}) copy-start(bf16[1280,640]{1,0:T(8,128)(2,1)} %param.15) | copy-start | bytes 4915204
where the time goes:
time: 143 us; the launch traced here: 142 us
  waiting for transfers between devices  39.2 us (27%)
  local copies, waits for them, and re-layouts  32.9 us (23%)
  starting transfers between devices  25.7 us (18%)
  other arithmetic  18.2 us (13%)
  blocking collectives  16.1 us (11%)
  matrix products  8.04 us (6%)
    all_to_all x1, waiting for transfers between devices, per_device(): lax.all_to_all(restored, 'lat', split_axis=0, concat_axis=2, tiled=True)  20.8 us
    all_to_all x1, blocking collectives, per_device(): lax.all_to_all(incoming, 'lon', split_axis=1, concat_axis=2, tiled=True)  16.1 us
    all_to_all x1, waiting for transfers between devices, per_device(): lax.all_to_all(coeffs, 'lat', split_axis=2, concat_axis=0, tiled=True)  13.8 us
    unnamed x81, local copies, waits for them, and re-layouts  13.6 us
    all_to_all x1, starting transfers between devices, per_device(): lax.all_to_all(coeffs, 'lat', split_axis=2, concat_axis=0, tiled=True)  7.3 us
    ppermute x2, starting transfers between devices, padded_2(): lax.ppermute(lax.slice_in_dim(block, block.shape[dim] - width, None, axis...  6.47 us
    slice x3, local copies, waits for them, and re-layouts, stencil_sum(): weights[row_shift * 5 + col_shift]  5.3 us
    all_to_all x1, starting transfers between devices, per_device(): lax.all_to_all(latent, 'lon', split_axis=2, concat_axis=1, tiled=True)  5.19 us
  transfers between devices with their start and end apart: 7, of which 3 were waited for; matrix products, arithmetic and copies ran while one was open for 10% of the time, Pallas kernels for 0%

commit v1 on v0

--- a/solution.py
+++ b/solution.py
@@ -1,6 +1,12 @@
+import functools
+import math
+
 import jax
 import jax.numpy as jnp
+import numpy as np
 from jax import lax
+from jax.experimental import pallas as pl
+from jax.experimental.pallas import tpu as pltpu
 from jax.sharding import PartitionSpec as P
 
 highest = lax.Precision.HIGHEST
@@ -146,9 +152,494 @@
     return channel_mlp(arrived, norm_gain, up_weight, down_weight)
 
 
+LANES = 128
+TILE = 8
+bf16 = jnp.bfloat16
+f32 = jnp.float32
+
+
+def legendre_numpy(modes, lat_count):
+    theta = np.pi * (np.arange(lat_count) + 0.5) / lat_count
+    cosine, sine = np.cos(theta), np.sin(theta)
+    table = np.zeros((modes, modes, lat_count))
+    for m in range(modes):
+        seed = 0.5 * (
+            math.log((2 * m + 1) / (4 * math.pi))
+            + math.lgamma(2 * m + 1)
+            - 2 * m * math.log(2.0)
+            - 2 * math.lgamma(m + 1)
+        )
+        table[m, m] = np.exp(seed + m * np.log(sine))
+        for l in range(m + 1, modes):
+            a = math.sqrt((4.0 * l * l - 1) / (l * l - m * m))
+            b = math.sqrt(max((l - 1.0) ** 2 - m * m, 0.0) / (4.0 * (l - 1.0) ** 2 - 1)) if l > 1 else 0.0
+            earlier = table[m, l - 2] if l > m + 1 else 0.0
+            table[m, l] = a * (cosine * table[m, l - 1] - b * earlier)
+    quadrature = 2 * np.pi**2 * sine / lat_count
+    return table, table * quadrature
+
+
+def split_numpy(table):
+    high = table.astype(np.float32).astype(jnp.bfloat16)
+    low = (table - high.astype(np.float64)).astype(np.float32).astype(jnp.bfloat16)
+    return np.stack([high, low])
+
+
+@functools.lru_cache(maxsize=None)
+def constant_tables(nl, nj, rows, cols, modes):
+    lat_count, lon_count = rows * nl, cols * nj
+    rs = rows // nj
+    pair = TILE // rs // 2
+    groups = modes // nl // pair
+    n = np.arange(lon_count)
+    k = np.arange(modes)
+    phase = 2 * np.pi * ((k[:, None] * n[None, :]) % lon_count) / lon_count
+    trig = np.stack([np.cos(phase), -np.sin(phase)], axis=1)
+    factor = np.where(k == 0, 1.0, 2.0)
+    same = np.eye(rs)
+    by_order = trig.reshape(nl, groups, pair, 2, lon_count)
+    forward = by_order.reshape(nl, groups, pair, 2, nj, cols) / lon_count
+    forward = np.einsum("lqopjn,rs->lqropjsn", forward, same)
+    forward = forward.reshape(modes * 2 * rs, nj * rs * cols)
+    wide = cols + 4
+    where = (np.arange(nj)[:, None] * cols + np.arange(wide)[None, :] - 2) % lon_count
+    back = (trig * factor[:, None, None]).reshape(nl, groups, pair, 2, lon_count)[..., where]
+    back = np.einsum("lqopjn,rs->jrnlqsop", back, same)
+    back = back.reshape(nj * rs * wide, modes * 2 * rs)
+    pick = np.zeros((nj, wide, lon_count))
+    pick[np.arange(nj)[:, None], np.arange(wide)[None, :], where] = 1.0
+    pick = np.einsum("jwtn,rs->jrwtsn", pick.reshape(nj, wide, nj, cols), same)
+    pick = pick.reshape(nj * rs * wide, nj * rs * cols)
+    table, weighted = legendre_numpy(modes, lat_count)
+
+    def by_lat(values):
+        parts = split_numpy(values)
+        parts = parts.reshape((2, nl, modes // nl) + values.shape[1:])
+        return np.moveaxis(parts, 1, 0)
+
+    return (
+        split_numpy(forward),
+        split_numpy(back),
+        pick.astype(jnp.bfloat16),
+        by_lat(weighted),
+        by_lat(np.swapaxes(table, 1, 2)),
+    )
+
+
+def halves(value):
+    high = value.astype(bf16)
+    return high, (value - high.astype(f32)).astype(bf16)
+
+
+def mm(a, b):
+    return jnp.dot(a, b, preferred_element_type=f32)
+
+
+def mm3(a_high, a_low, b):
+    high, low = halves(b)
+    return mm(a_high, high) + (mm(a_high, low) + mm(a_low, high))
+
+
+def stencil_block(source, taps, cols, rows, width):
+    totals = [None] * rows
+    for r in range(rows + 4):
+        base = source[r, :, cols]
+        for b in range(5):
+            moved = base if b == 0 else pltpu.roll(base, base.shape[0] - b, 0)
+            for a in range(5):
+                i = r - a
+                if 0 <= i < rows:
+                    term = taps[a * 5 + b : a * 5 + b + 1, cols] * moved
+                    if a == 2 and b == 2:
+                        term = term + moved
+                    totals[i] = term if totals[i] is None else totals[i] + term
+    return [total[:width] for total in totals]
+
+
+def block_kernel(
+    nl, nj,
+    latent, taps1, taps2, gains, norm_gain, fwd, back, pick, up_hbm, down_hbm, wt_hbm, pt_hbm,
+    out,
+    row_in, west_out, east_out, west_in, east_in, first_pad, mine, circle, sent_c, spec_in,
+    spec_out, got_c, wide_out, second_pad, gain_in, gain_all, third, up, down, wt, pt,
+    load_sem, row_s, row_r, col_s, col_r, gain_s, gain_r, a_s, a_r, c_s, c_r, b_s, b_r, z_s, z_r,
+    halo_s, halo_r,
+):
+    rows, cols, channels = latent.shape
+    wide = cols + 4
+    blocks = channels // LANES
+    rs = rows // nj
+    part = rs * cols
+    total = nl * nj
+    per = spec_in.shape[0]
+    orders = wt.shape[1]
+    pair = TILE // rs // 2
+    groups = orders // pair
+    units = groups * blocks
+    lat_count = rows * nl
+    la, lo = lax.axis_index("lat"), lax.axis_index("lon")
+    me = la * nj + lo
+    above, below = lax.rem(la + nl - 1, nl), lax.rem(la + 1, nl)
+    right, left = lax.rem(lo + 1, nj), lax.rem(lo + nj - 1, nj)
+    has_above, has_below = la > 0, la < nl - 1
+
+    def span(start, size):
+        return pl.ds(start if isinstance(start, int) else pl.multiple_of(start, TILE), size)
+
+    def lanes(block):
+        return pl.ds(block * LANES, LANES)
+
+    def rcopy(src, dst, send, recv, a, b):
+        return pltpu.make_async_remote_copy(
+            src_ref=src, dst_ref=dst, send_sem=send, recv_sem=recv,
+            device_id={"lat": a, "lon": b}, device_id_type=pl.DeviceIdType.MESH,
+        )
+
+    loads = [
+        pltpu.make_async_copy(wt_hbm.at[la], wt, load_sem.at[0]),
+        pltpu.make_async_copy(pt_hbm.at[la], pt, load_sem.at[1]),
+        pltpu.make_async_copy(up_hbm, up, load_sem.at[2]),
+        pltpu.make_async_copy(down_hbm, down, load_sem.at[3]),
+    ]
+    for load in loads:
+        load.start()
+
+    barrier = pltpu.get_barrier_semaphore()
+
+    def greet(d, carry):
+        peer = lax.rem(me + d, total)
+        pl.semaphore_signal(
+            barrier, inc=1, device_id={"lat": peer // nj, "lon": lax.rem(peer, nj)},
+            device_id_type=pl.DeviceIdType.MESH,
+        )
+        return carry
+
+    lax.fori_loop(1, total, greet, 0)
+    for i in range(rows):
+        west_out[i] = latent[i, 0:2, :]
+        east_out[i] = latent[i, cols - 2 : cols, :]
+    pl.semaphore_wait(barrier, total - 1)
+
+    halos = [
+        (has_below, has_above,
+         rcopy(latent.at[pl.ds(rows - 2, 2)], row_in.at[0], row_s.at[0], row_r.at[0], below, lo)),
+        (has_above, has_below,
+         rcopy(latent.at[pl.ds(0, 2)], row_in.at[1], row_s.at[1], row_r.at[1], above, lo)),
+    ]
+    for side, (source, target, to) in enumerate(((east_out, west_in, right), (west_out, east_in, left))):
+        s, r = col_s.at[side], col_r.at[side]
+        halos += [
+            (None, None, rcopy(source, target.at[pl.ds(2, rows)], s.at[0], r.at[0], la, to)),
+            (has_below, has_above,
+             rcopy(source.at[pl.ds(rows - 2, 2)], target.at[pl.ds(0, 2)], s.at[1], r.at[1], below, to)),
+            (has_above, has_below,
+             rcopy(source.at[pl.ds(0, 2)], target.at[pl.ds(rows + 2, 2)], s.at[2], r.at[2], above, to)),
+        ]
+
+    def guarded(guard, action):
+        if guard is None:
+            action()
+        else:
+            pl.when(guard)(action)
+
+    for send, _, copy in halos:
+        guarded(send, copy.start)
+    gain_copies = []
+    for d in range(1, nj):
+        gain_copies.append(
+            rcopy(gains, gain_in.at[lo], gain_s.at[d], gain_r.at[d], la, lax.rem(lo + d, nj))
+        )
+    for copy in gain_copies:
+        copy.start()
+    gain_in[lo] = gains[...]
+    first_pad[2 : rows + 2, 2 : cols + 2, :] = latent[...]
+    blank = jnp.zeros((2, wide, channels), f32)
+    for absent, place in ((la == 0, pl.ds(0, 2)), (la == nl - 1, pl.ds(rows + 2, 2))):
+        @pl.when(absent)
+        def _(place=place):
+            first_pad[place] = blank
+            second_pad[place] = blank
+    for _, arrive, copy in halos:
+        guarded(arrive, copy.wait_recv)
+    for side, (guard, base) in enumerate(((has_above, 0), (has_below, rows + 2))):
+        @pl.when(guard)
+        def _(side=side, base=base):
+            for i in range(2):
+                first_pad[base + i, 2 : cols + 2, :] = row_in[side, i]
+                first_pad[base + i, 0:2, :] = west_in[base + i]
+                first_pad[base + i, cols + 2 : wide, :] = east_in[base + i]
+    for i in range(rows):
+        first_pad[2 + i, 0:2, :] = west_in[2 + i]
+        first_pad[2 + i, cols + 2 : wide, :] = east_in[2 + i]
+
+    def a_copy(block, d):
+        to = lax.rem(lo + d, nj)
+        return rcopy(
+            mine.at[span(to * part, part), lanes(block)], circle.at[lo, :, lanes(block)],
+            a_s.at[block, d], a_r.at[block, d], la, to,
+        )
+
+    def z_copy(block, d):
+        to = lax.rem(lo + d, nj)
+        return rcopy(
+            wide_out.at[pl.ds(to * rs, rs), :, lanes(block)],
+            second_pad.at[pl.ds(2 + lo * rs, rs), :, lanes(block)],
+            z_s.at[block, d], z_r.at[block, d], la, to,
+        )
+
+    def c_copy(a, b):
+        peer = a * nj + b
+        return rcopy(
+            sent_c.at[a, pl.ds(per * b, per)], spec_in.at[:, span(me * TILE, TILE), :],
+            c_s.at[peer], c_r.at[me], a, b,
+        )
+
+    def c_arrival(peer, a, b):
+        return rcopy(
+            sent_c.at[a, pl.ds(per * b, per)], spec_in.at[:, span(peer * TILE, TILE), :],
+            c_s.at[peer], c_r.at[peer], a, b,
+        )
+
+    def b_copy(a, b):
+        peer = a * nj + b
+        return rcopy(
+            spec_out.at[:, span(peer * TILE, TILE), :], got_c.at[la, pl.ds(per * lo, per)],
+            b_s.at[peer], b_r.at[me], a, b,
+        )
+
+    def b_arrival(peer, a, b):
+        return rcopy(
+            spec_out.at[:, span(peer * TILE, TILE), :], got_c.at[a, pl.ds(per * b, per)],
+            b_s.at[peer], b_r.at[peer], a, b,
+        )
+
+    for block in range(blocks):
+        sums = stencil_block(first_pad, taps1, lanes(block), rows, cols)
+        for i in range(rows):
+            mine[cols * i : cols * (i + 1), lanes(block)] = sums[i][:cols]
+        for d in range(1, nj):
+            a_copy(block, d).start()
+        circle[lo, :, lanes(block)] = mine[span(lo * part, part), lanes(block)]
+
+    if per * nj > units:
+        sent_c[:, units:] = jnp.zeros((nl, per * nj - units, TILE, LANES), f32)
+    for block in range(blocks):
+        for d in range(1, nj):
+            a_copy(block, d).wait_recv()
+        values = circle[:, :, lanes(block)].reshape(nj * part, LANES)
+        coeffs = mm3(fwd[0], fwd[1], values)
+        sent_c[:, block * groups : (block + 1) * groups] = coeffs.reshape(nl, groups, TILE, LANES)
+        for b in range(nj):
+            if (min(per * (b + 1), units) - 1) // groups == block:
+                def send_lat(d, carry, b=b):
+                    a = lax.rem(la + d, nl)
+
+                    @pl.when(a * nj + b != me)
+                    def _():
+                        c_copy(a, b).start()
+                    return carry
+
+                lax.fori_loop(0, nl, send_lat, 0)
+
+    spec_in[:, span(me * TILE, TILE), :] = sent_c[la, pl.ds(per * lo, per)]
+    for copy in gain_copies:
+        copy.wait_recv()
+    width = gains.shape[1]
+    for j in range(nj):
+        gain_all[:, width * j : width * (j + 1)] = gain_in[j]
+    loads[0].wait()
+    loads[1].wait()
+
+    def take_c(peer, carry):
+        @pl.when(peer != me)
+        def _():
+            c_arrival(peer, peer // nj, lax.rem(peer, nj)).wait_recv()
+        return carry
+
+    lax.fori_loop(0, total, take_c, 0)
+
+    for t in range(per):
+        unit = per * lo + t
+        block = jnp.minimum(unit // groups, blocks - 1)
+        group = lax.rem(unit, groups)
+        gain = gain_all[:, pl.ds(pl.multiple_of(block * LANES, LANES), LANES)]
+        gain = jnp.concatenate([gain, gain], axis=1)
+        for o in range(pair):
+            data = jnp.concatenate(
+                [spec_in[t, pl.ds(2 * o + ri, lat_count, stride=2 * pair), :] for ri in range(2)], axis=1
+            )
+            order = group * pair + o
+            spectrum = mm3(wt[0, order], wt[1, order], data) * gain
+            restored = mm3(pt[0, order], pt[1, order], spectrum)
+            for ri in range(2):
+                spec_out[t, pl.ds(2 * o + ri, lat_count, stride=2 * pair), :] = (
+                    restored[:, ri * LANES : (ri + 1) * LANES]
+                )
+
+    def send_b(d, carry):
+        peer = lax.rem(me + d, total)
+        b_copy(peer // nj, lax.rem(peer, nj)).start()
+        return carry
+
+    lax.fori_loop(1, total, send_b, 0)
+    got_c[la, pl.ds(per * lo, per)] = spec_out[:, span(me * TILE, TILE), :]
+
+    taken = set()
+    for block in range(blocks):
+        for unit in range(block * groups, (block + 1) * groups):
+            b = unit // per
+            if b not in taken:
+                taken.add(b)
+
+                def take_b(a, carry, b=b):
+                    @pl.when(a * nj + b != me)
+                    def _():
+                        b_arrival(a * nj + b, a, b).wait_recv()
+                    return carry
+
+                lax.fori_loop(0, nl, take_b, 0)
+        coeffs = got_c[:, block * groups : (block + 1) * groups].reshape(nl * groups * TILE, LANES)
+        values = circle[:, :, lanes(block)].reshape(nj * part, LANES)
+        high, low = halves(values)
+        rebuilt = mm3(back[0], back[1], coeffs) + (mm(pick[...], low) + mm(pick[...], high))
+        wide_out[:, :, lanes(block)] = rebuilt.reshape(nj * rs, wide, LANES)
+        for d in range(1, nj):
+            z_copy(block, d).start()
+        second_pad[pl.ds(2 + lo * rs, rs), :, lanes(block)] = wide_out[pl.ds(lo * rs, rs), :, lanes(block)]
+
+    def row_copies(block):
+        edge = second_pad.at[:, :, lanes(block)]
+        return (
+            (has_below, has_above,
+             rcopy(edge.at[pl.ds(rows, 2)], edge.at[pl.ds(0, 2)], halo_s.at[block, 0], halo_r.at[block, 0], below, lo)),
+            (has_above, has_below,
+             rcopy(edge.at[pl.ds(2, 2)], edge.at[pl.ds(rows + 2, 2)], halo_s.at[block, 1], halo_r.at[block, 1], above, lo)),
+        )
+
+    for block in range(blocks):
+        for d in range(1, nj):
+            z_copy(block, d).wait_recv()
+        for send, _, copy in row_copies(block):
+            guarded(send, copy.start)
+    for block in range(blocks):
+        for _, arrive, copy in row_copies(block):
+            guarded(arrive, copy.wait_recv)
+        sums = stencil_block(second_pad, taps2, lanes(block), rows, cols)
+        for i in range(rows):
+            third[cols * i : cols * (i + 1), lanes(block)] = sums[i][:cols]
+
+    loads[2].wait()
+    loads[3].wait()
+    state = third[...]
+    average = jnp.mean(state, axis=-1, keepdims=True)
+    centred = state - average
+    spread = jnp.mean(centred * centred, axis=-1, keepdims=True)
+    normed = (centred * lax.rsqrt(spread + 1e-05) * norm_gain[...]).astype(bf16)
+    active = jax.nn.gelu(mm(normed, up[...]), approximate=True).astype(bf16)
+    third[...] = state + mm(active, down[...])
+    for i in range(rows):
+        out[i] = third[cols * i : cols * (i + 1), :]
+
+    for send, _, copy in halos:
+        guarded(send, copy.wait_send)
+    for copy in gain_copies:
+        copy.wait_send()
+    for block in range(blocks):
+        for d in range(1, nj):
+            a_copy(block, d).wait_send()
+            z_copy(block, d).wait_send()
+        for send, _, copy in row_copies(block):
+            guarded(send, copy.wait_send)
+
+    def finish(peer, carry):
+        @pl.when(peer != me)
+        def _():
+            a, b = peer // nj, lax.rem(peer, nj)
+            c_copy(a, b).wait_send()
+            b_copy(a, b).wait_send()
+        return carry
+
+    lax.fori_loop(0, total, finish, 0)
+
+
+def fused(nl, nj, latent, conv_first, conv_second, filter_gains, norm_gain, up_weight, down_weight):
+    rows, cols, channels = latent.shape
+    modes, width = filter_gains.shape
+    forward, back, pick, wt, pt = (jnp.asarray(t) for t in constant_tables(nl, nj, rows, cols, modes))
+    rs = rows // nj
+    wide = cols + 4
+    blocks = channels // LANES
+    total = nl * nj
+    groups = modes // nl // (TILE // rs // 2)
+    per = -(-groups * blocks // nj)
+    vm = lambda *shape, kind=f32: pltpu.VMEM(shape, kind)
+    dma = lambda *shape: pltpu.SemaphoreType.DMA(shape)
+    here = pl.BlockSpec(memory_space=pltpu.VMEM)
+    far = pl.BlockSpec(memory_space=pltpu.HBM)
+    return pl.pallas_call(
+        functools.partial(block_kernel, nl, nj),
+        out_shape=jax.ShapeDtypeStruct(latent.shape, f32),
+        in_specs=[here] * 8 + [far] * 4,
+        out_specs=here,
+        scratch_shapes=[
+            vm(2, 2, cols, channels),
+            vm(rows, 2, channels),
+            vm(rows, 2, channels),
+            vm(rows + 4, 2, channels),
+            vm(rows + 4, 2, channels),
+            vm(rows + 4, wide, channels),
+            vm(rows * cols, channels),
+            vm(nj, rs * cols, channels),
+            vm(nl, per * nj, TILE, LANES),
+            vm(per, total * TILE, LANES),
+            vm(per, total * TILE, LANES),
+            vm(nl, per * nj, TILE, LANES),
+            vm(nj * rs, wide, channels),
+            vm(rows + 4, wide, channels),
+            vm(nj, modes, width),
+            vm(modes, channels),
+            vm(rows * cols, channels),
+            vm(*up_weight.shape, kind=bf16),
+            vm(*down_weight.shape, kind=bf16),
+            vm(*wt.shape[1:], kind=bf16),
+            vm(*pt.shape[1:], kind=bf16),
+            dma(4),
+            dma(2), dma(2), dma(2, 3), dma(2, 3), dma(nj), dma(nj),
+            dma(blocks, nj), dma(blocks, nj), dma(total), dma(total), dma(total), dma(total),
+            dma(blocks, nj), dma(blocks, nj), dma(blocks, 2), dma(blocks, 2),
+        ],
+        compiler_params=pltpu.CompilerParams(
+            collective_id=0, has_side_effects=True, vmem_limit_bytes=60 * 1024 * 1024
+        ),
+        name="block",
+    )(
+        latent, conv_first, conv_second, filter_gains, norm_gain[None, :], forward, back, pick,
+        up_weight, down_weight, wt, pt,
+    )
+
+
+def fits(nl, nj, latent, filter_gains):
+    rows, cols, channels = latent.shape
+    modes = filter_gains.shape[0]
+    if rows % nj or channels % LANES or modes % nl or nj < 2 or nl < 2:
+        return False
+    rs = rows // nj
+    if TILE % (2 * rs) or (rs * cols) % TILE or (cols + 4) % TILE:
+        return False
+    return (modes // nl) % (TILE // rs // 2) == 0
+
+
+def body(latent, conv_first, conv_second, filter_gains, norm_gain, up_weight, down_weight):
+    nl, nj = lax.axis_size("lat"), lax.axis_size("lon")
+    arguments = (latent, conv_first, conv_second, filter_gains, norm_gain, up_weight, down_weight)
+    if fits(nl, nj, latent, filter_gains):
+        return fused(nl, nj, *arguments)
+    return per_device(*arguments)
+
+
 def solution(mesh):
     return jax.shard_map(
-        per_device,
+        body,
         mesh=mesh,
         in_specs=(P("lat", "lon", None), P(), P(), P(None, "lon"), P(), P(), P()),
         out_specs=P("lat", "lon", None),

time: 143 us -> 66.7 us (0.47)
  the two profiles are of different devices: /device:TPU:0 before, /device:TPU:19 now
where the time goes in v1:
time: 66.7 us; the launch traced here: 66.5 us
  Pallas kernels  60.9 us (91%)
  local copies, waits for them, and re-layouts  5.5 us (8%)
    pallas_call x1, Pallas kernels, fused(): pl.pallas_call(functools.partial(block_kernel, nl, nj), out_shape=jax.Sha...  60.9 us
    pallas_call x1, local copies, waits for them, and re-layouts, fused(): pl.pallas_call(functools.partial(block_kernel, nl, nj), out_shape=jax.Sha...  2.23 us
    unnamed x1, local copies, waits for them, and re-layouts  2.01 us

profile of v1, /device:TPU:19, one launch (start us, length us, event | category | flops | bytes accessed | tf_op | source)
XLA Modules:
  0.0 66.5 jit_solution(15046148862400977489)
XLA Ops:
  0.0 1.3 %broadcast_in_dim.3.norm_gain = f32[1,640]{1,0:T(1,128)} reshape(f32[640]{0:T(1024)} %param.16) | data formatting | bytes 5120 | tf_op jit(solution)/shard_map/broadcast_in_dim | solution.py:616
  1.3 2.0 %copy.13.latent = f32[8,28,640]{2,1,0:T(8,128)} copy(f32[8,28,640]{2,0,1:T(8,128)} %param.12) | data formatting | bytes 1146880 | tf_op args[0]
  3.3 60.9 %block.1 = f32[8,28,640]{2,1,0:T(8,128)} custom-call(f32[8,28,640]{2,1,0:T(8,128)} %copy.13.latent, f32[25,640]{1,0:T(8,128)} %taps1.1, f32[25,640]{1,0:T(8,128)} %taps2.1, f32[48,160]{1,0:T(8,128)} %gains.1, f32[1,640]{1,0:T(1,128)} %broadcast_in_dim.3.norm_gain, bf16[2,192,224]{2,1,0:T(8,128)(2,1)} %constant.10.clone.fwd, ...), custom_call_target="tpu_custom_call" | custom-call | tf_op jit(solution)/shard_map/block/pallas_call | solution.py:579
  64.2 2.2 %copy.14 = f32[8,28,640]{2,0,1:T(8,128)} copy(f32[8,28,640]{2,1,0:T(8,128)} %block.1) | data formatting | bytes 1146880 | tf_op jit(solution)/shard_map/block/pallas_call | solution.py:579

commit v2 on v1

--- a/solution.py
+++ b/solution.py
@@ -213,9 +213,10 @@
     table, weighted = legendre_numpy(modes, lat_count)
 
     def by_lat(values):
-        parts = split_numpy(values)
-        parts = parts.reshape((2, nl, modes // nl) + values.shape[1:])
-        return np.moveaxis(parts, 1, 0)
+        room = -values.shape[2] % (LANES // 2)
+        parts = split_numpy(np.pad(values, ((0, 0), (0, 0), (0, room))))
+        parts = np.concatenate([parts[0], parts[1]], axis=-1)
+        return parts.reshape((nl, modes // nl) + parts.shape[1:])
 
     return (
         split_numpy(forward),
@@ -238,6 +239,18 @@
 def mm3(a_high, a_low, b):
     high, low = halves(b)
     return mm(a_high, high) + (mm(a_high, low) + mm(a_low, high))
+
+
+def mm_packed(table, value):
+    depth = table.shape[1] // 2
+    if value.shape[0] < depth:
+        blank = jnp.zeros((depth - value.shape[0], value.shape[1]), f32)
+        value = jnp.concatenate([value, blank], axis=0)
+    high, low = halves(value)
+    return mm(
+        jnp.concatenate([table, table[:, :depth]], axis=1),
+        jnp.concatenate([high, high, low], axis=0),
+    )
 
 
 def stencil_block(source, taps, cols, rows, width):
@@ -257,22 +270,23 @@
 
 
 def block_kernel(
-    nl, nj,
+    nl, nj, rows,
     latent, taps1, taps2, gains, norm_gain, fwd, back, pick, up_hbm, down_hbm, wt_hbm, pt_hbm,
     out,
-    row_in, west_out, east_out, west_in, east_in, first_pad, mine, circle, sent_c, spec_in,
+    grid, row_out, row_in, west_out, east_out, west_in, east_in, first_pad, mine, circle, sent_c, spec_in,
     spec_out, got_c, wide_out, second_pad, gain_in, gain_all, third, up, down, wt, pt,
-    load_sem, row_s, row_r, col_s, col_r, gain_s, gain_r, a_s, a_r, c_s, c_r, b_s, b_r, z_s, z_r,
+    load_sem, in_sem, out_sem, row_s, row_r, col_s, col_r, gain_s, gain_r, a_s, a_r, c_s, c_r, b_s, b_r, z_s, z_r,
     halo_s, halo_r,
 ):
-    rows, cols, channels = latent.shape
+    channels = latent.shape[1]
+    cols = latent.shape[0] // rows
     wide = cols + 4
     blocks = channels // LANES
     rs = rows // nj
     part = rs * cols
     total = nl * nj
     per = spec_in.shape[0]
-    orders = wt.shape[1]
+    orders = wt.shape[0]
     pair = TILE // rs // 2
     groups = orders // pair
     units = groups * blocks
@@ -301,6 +315,15 @@
         pltpu.make_async_copy(up_hbm, up, load_sem.at[2]),
         pltpu.make_async_copy(down_hbm, down, load_sem.at[3]),
     ]
+
+    def in_copy(block):
+        return pltpu.make_async_copy(latent.at[:, lanes(block)], grid.at[block], in_sem.at[block])
+
+    def out_copy(block):
+        return pltpu.make_async_copy(grid.at[block], out.at[:, lanes(block)], out_sem.at[block])
+
+    for block in range(blocks):
+        in_copy(block).start()
     for load in loads:
         load.start()
 
@@ -315,16 +338,30 @@
         return carry
 
     lax.fori_loop(1, total, greet, 0)
-    for i in range(rows):
-        west_out[i] = latent[i, 0:2, :]
-        east_out[i] = latent[i, cols - 2 : cols, :]
+    for block in range(blocks):
+        in_copy(block).wait()
+        for i in range(rows):
+            line = grid[block, pl.ds(i, cols, stride=rows), :]
+            first_pad[2 + i, 2 : cols + 2, lanes(block)] = line
+            west_out[i, :, lanes(block)] = line[:2]
+            east_out[i, :, lanes(block)] = line[cols - 2 :]
+            if i < 2:
+                row_out[1, i, :, lanes(block)] = line
+            if i >= rows - 2:
+                row_out[0, i - rows + 2, :, lanes(block)] = line
+    blank = jnp.zeros((2, wide, channels), f32)
+    for absent, place in ((la == 0, pl.ds(0, 2)), (la == nl - 1, pl.ds(rows + 2, 2))):
+        @pl.when(absent)
+        def _(place=place):
+            first_pad[place] = blank
+            second_pad[place] = blank
     pl.semaphore_wait(barrier, total - 1)
 
     halos = [
         (has_below, has_above,
-         rcopy(latent.at[pl.ds(rows - 2, 2)], row_in.at[0], row_s.at[0], row_r.at[0], below, lo)),
+         rcopy(row_out.at[0], row_in.at[0], row_s.at[0], row_r.at[0], below, lo)),
         (has_above, has_below,
-         rcopy(latent.at[pl.ds(0, 2)], row_in.at[1], row_s.at[1], row_r.at[1], above, lo)),
+         rcopy(row_out.at[1], row_in.at[1], row_s.at[1], row_r.at[1], above, lo)),
     ]
     for side, (source, target, to) in enumerate(((east_out, west_in, right), (west_out, east_in, left))):
         s, r = col_s.at[side], col_r.at[side]
@@ -352,13 +389,6 @@
     for copy in gain_copies:
         copy.start()
     gain_in[lo] = gains[...]
-    first_pad[2 : rows + 2, 2 : cols + 2, :] = latent[...]
-    blank = jnp.zeros((2, wide, channels), f32)
-    for absent, place in ((la == 0, pl.ds(0, 2)), (la == nl - 1, pl.ds(rows + 2, 2))):
-        @pl.when(absent)
-        def _(place=place):
-            first_pad[place] = blank
-            second_pad[place] = blank
     for _, arrive, copy in halos:
         guarded(arrive, copy.wait_recv)
     for side, (guard, base) in enumerate(((has_above, 0), (has_below, rows + 2))):
@@ -387,31 +417,41 @@
             z_s.at[block, d], z_r.at[block, d], la, to,
         )
 
-    def c_copy(a, b):
+    def c_copy(t, a, b, source):
+        return rcopy(
+            sent_c.at[a, nj * t + b], spec_in.at[t, span(source * TILE, TILE), :],
+            c_s.at[t, a * nj + b], c_r.at[t, source], a, b,
+        )
+
+    def b_copy(t, a, b, la, lo):
         peer = a * nj + b
         return rcopy(
-            sent_c.at[a, pl.ds(per * b, per)], spec_in.at[:, span(me * TILE, TILE), :],
-            c_s.at[peer], c_r.at[me], a, b,
-        )
-
-    def c_arrival(peer, a, b):
-        return rcopy(
-            sent_c.at[a, pl.ds(per * b, per)], spec_in.at[:, span(peer * TILE, TILE), :],
-            c_s.at[peer], c_r.at[peer], a, b,
-        )
-
-    def b_copy(a, b):
-        peer = a * nj + b
-        return rcopy(
-            spec_out.at[:, span(peer * TILE, TILE), :], got_c.at[la, pl.ds(per * lo, per)],
-            b_s.at[peer], b_r.at[me], a, b,
-        )
-
-    def b_arrival(peer, a, b):
-        return rcopy(
-            spec_out.at[:, span(peer * TILE, TILE), :], got_c.at[a, pl.ds(per * b, per)],
-            b_s.at[peer], b_r.at[peer], a, b,
-        )
+            spec_out.at[t, span(peer * TILE, TILE), :], got_c.at[la, nj * t + lo],
+            b_s.at[t, peer], b_r.at[t, la * nj + lo], a, b,
+        )
+
+    def keep_c(t):
+        spec_in[t, span(me * TILE, TILE), :] = sent_c[la, nj * t + lo]
+
+    def others(action):
+        def step(d, carry):
+            peer = lax.rem(me + d, total)
+            action(peer, peer // nj, lax.rem(peer, nj))
+            return carry
+
+        lax.fori_loop(1, total, step, 0)
+
+    def own_unit(t, action):
+        if nj * t + nj <= units:
+            action()
+        else:
+            pl.when(nj * t + lo < units)(action)
+
+    def real_unit(t, b, action):
+        if nj * t + nj <= units:
+            action()
+        else:
+            pl.when(nj * t + b < units)(action)
 
     for block in range(blocks):
         sums = stencil_block(first_pad, taps1, lanes(block), rows, cols)
@@ -421,27 +461,17 @@
             a_copy(block, d).start()
         circle[lo, :, lanes(block)] = mine[span(lo * part, part), lanes(block)]
 
-    if per * nj > units:
-        sent_c[:, units:] = jnp.zeros((nl, per * nj - units, TILE, LANES), f32)
     for block in range(blocks):
         for d in range(1, nj):
             a_copy(block, d).wait_recv()
         values = circle[:, :, lanes(block)].reshape(nj * part, LANES)
         coeffs = mm3(fwd[0], fwd[1], values)
         sent_c[:, block * groups : (block + 1) * groups] = coeffs.reshape(nl, groups, TILE, LANES)
-        for b in range(nj):
-            if (min(per * (b + 1), units) - 1) // groups == block:
-                def send_lat(d, carry, b=b):
-                    a = lax.rem(la + d, nl)
-
-                    @pl.when(a * nj + b != me)
-                    def _():
-                        c_copy(a, b).start()
-                    return carry
-
-                lax.fori_loop(0, nl, send_lat, 0)
-
-    spec_in[:, span(me * TILE, TILE), :] = sent_c[la, pl.ds(per * lo, per)]
+        for t in range(per):
+            if (min(nj * (t + 1), units) - 1) // groups == block:
+                others(lambda peer, a, b, t=t: real_unit(t, b, c_copy(t, a, b, me).start))
+                own_unit(t, lambda t=t: keep_c(t))
+
     for copy in gain_copies:
         copy.wait_recv()
     width = gains.shape[1]
@@ -450,17 +480,10 @@
     loads[0].wait()
     loads[1].wait()
 
-    def take_c(peer, carry):
-        @pl.when(peer != me)
-        def _():
-            c_arrival(peer, peer // nj, lax.rem(peer, nj)).wait_recv()
-        return carry
-
-    lax.fori_loop(0, total, take_c, 0)
-
-    for t in range(per):
-        unit = per * lo + t
-        block = jnp.minimum(unit // groups, blocks - 1)
+    def filter_unit(t):
+        others(lambda peer, a, b: c_copy(t, la, lo, peer).wait_recv())
+        unit = nj * t + lo
+        block = unit // groups
         group = lax.rem(unit, groups)
         gain = gain_all[:, pl.ds(pl.multiple_of(block * LANES, LANES), LANES)]
         gain = jnp.concatenate([gain, gain], axis=1)
@@ -469,35 +492,24 @@
                 [spec_in[t, pl.ds(2 * o + ri, lat_count, stride=2 * pair), :] for ri in range(2)], axis=1
             )
             order = group * pair + o
-            spectrum = mm3(wt[0, order], wt[1, order], data) * gain
-            restored = mm3(pt[0, order], pt[1, order], spectrum)
+            restored = mm_packed(pt[order], mm_packed(wt[order], data) * gain)
             for ri in range(2):
                 spec_out[t, pl.ds(2 * o + ri, lat_count, stride=2 * pair), :] = (
                     restored[:, ri * LANES : (ri + 1) * LANES]
                 )
-
-    def send_b(d, carry):
-        peer = lax.rem(me + d, total)
-        b_copy(peer // nj, lax.rem(peer, nj)).start()
-        return carry
-
-    lax.fori_loop(1, total, send_b, 0)
-    got_c[la, pl.ds(per * lo, per)] = spec_out[:, span(me * TILE, TILE), :]
+        others(lambda peer, a, b: b_copy(t, a, b, la, lo).start())
+        got_c[la, nj * t + lo] = spec_out[t, span(me * TILE, TILE), :]
+
+    for t in range(per):
+        own_unit(t, lambda t=t: filter_unit(t))
 
     taken = set()
     for block in range(blocks):
         for unit in range(block * groups, (block + 1) * groups):
-            b = unit // per
-            if b not in taken:
-                taken.add(b)
-
-                def take_b(a, carry, b=b):
-                    @pl.when(a * nj + b != me)
-                    def _():
-                        b_arrival(a * nj + b, a, b).wait_recv()
-                    return carry
-
-                lax.fori_loop(0, nl, take_b, 0)
+            t = unit // nj
+            if t not in taken:
+                taken.add(t)
+                others(lambda peer, a, b, t=t: real_unit(t, b, b_copy(t, la, lo, a, b).wait_recv))
         coeffs = got_c[:, block * groups : (block + 1) * groups].reshape(nl * groups * TILE, LANES)
         values = circle[:, :, lanes(block)].reshape(nj * part, LANES)
         high, low = halves(values)
@@ -534,12 +546,16 @@
     average = jnp.mean(state, axis=-1, keepdims=True)
     centred = state - average
     spread = jnp.mean(centred * centred, axis=-1, keepdims=True)
-    normed = (centred * lax.rsqrt(spread + 1e-05) * norm_gain[...]).astype(bf16)
+    normed = (centred * lax.rsqrt(spread + 1e-05) * norm_gain[...].reshape(1, channels)).astype(bf16)
     active = jax.nn.gelu(mm(normed, up[...]), approximate=True).astype(bf16)
     third[...] = state + mm(active, down[...])
-    for i in range(rows):
-        out[i] = third[cols * i : cols * (i + 1), :]
-
+    for block in range(blocks):
+        for i in range(rows):
+            grid[block, pl.ds(i, cols, stride=rows), :] = third[cols * i : cols * (i + 1), lanes(block)]
+        out_copy(block).start()
+
+    for block in range(blocks):
+        out_copy(block).wait()
     for send, _, copy in halos:
         guarded(send, copy.wait_send)
     for copy in gain_copies:
@@ -551,15 +567,9 @@
         for send, _, copy in row_copies(block):
             guarded(send, copy.wait_send)
 
-    def finish(peer, carry):
-        @pl.when(peer != me)
-        def _():
-            a, b = peer // nj, lax.rem(peer, nj)
-            c_copy(a, b).wait_send()
-            b_copy(a, b).wait_send()
-        return carry
-
-    lax.fori_loop(0, total, finish, 0)
+    for t in range(per):
+        others(lambda peer, a, b, t=t: real_unit(t, b, c_copy(t, a, b, me).wait_send))
+        own_unit(t, lambda t=t: others(lambda peer, a, b: b_copy(t, a, b, la, lo).wait_send()))
 
 
 def fused(nl, nj, latent, conv_first, conv_second, filter_gains, norm_gain, up_weight, down_weight):
@@ -576,12 +586,14 @@
     dma = lambda *shape: pltpu.SemaphoreType.DMA(shape)
     here = pl.BlockSpec(memory_space=pltpu.VMEM)
     far = pl.BlockSpec(memory_space=pltpu.HBM)
-    return pl.pallas_call(
-        functools.partial(block_kernel, nl, nj),
-        out_shape=jax.ShapeDtypeStruct(latent.shape, f32),
-        in_specs=[here] * 8 + [far] * 4,
-        out_specs=here,
+    result = pl.pallas_call(
+        functools.partial(block_kernel, nl, nj, rows),
+        out_shape=jax.ShapeDtypeStruct((cols * rows, channels), f32),
+        in_specs=[far] + [here] * 7 + [far] * 4,
+        out_specs=far,
         scratch_shapes=[
+            vm(blocks, cols * rows, LANES),
+            vm(2, 2, cols, channels),
             vm(2, 2, cols, channels),
             vm(rows, 2, channels),
             vm(rows, 2, channels),
@@ -603,9 +615,9 @@
             vm(*down_weight.shape, kind=bf16),
             vm(*wt.shape[1:], kind=bf16),
             vm(*pt.shape[1:], kind=bf16),
-            dma(4),
+            dma(4), dma(blocks), dma(blocks),
             dma(2), dma(2), dma(2, 3), dma(2, 3), dma(nj), dma(nj),
-            dma(blocks, nj), dma(blocks, nj), dma(total), dma(total), dma(total), dma(total),
+            dma(blocks, nj), dma(blocks, nj), dma(per, total), dma(per, total), dma(per, total), dma(per, total),
             dma(blocks, nj), dma(blocks, nj), dma(blocks, 2), dma(blocks, 2),
         ],
         compiler_params=pltpu.CompilerParams(
@@ -613,9 +625,10 @@
         ),
         name="block",
     )(
-        latent, conv_first, conv_second, filter_gains, norm_gain[None, :], forward, back, pick,
-        up_weight, down_weight, wt, pt,
+        jnp.swapaxes(latent, 0, 1).reshape(cols * rows, channels), conv_first, conv_second,
+        filter_gains, norm_gain, forward, back, pick, up_weight, down_weight, wt, pt,
     )
+    return jnp.swapaxes(result.reshape(cols, rows, channels), 0, 1)
 
 
 def fits(nl, nj, latent, filter_gains):
@@ -626,6 +639,8 @@
     rs = rows // nj
     if TILE % (2 * rs) or (rs * cols) % TILE or (cols + 4) % TILE:
         return False
+    if modes > LANES // 2 or rows * nl > LANES // 2:
+        return False
     return (modes // nl) % (TILE // rs // 2) == 0
 
 

time: 66.7 us -> 64.4 us (0.966)
  local copies, waits for them, and re-layouts: 5.5 us -> 1.91 us
  Pallas kernels: 60.9 us -> 62.3 us
    pallas_call x1 -> x0, local copies, waits for them, and re-layouts: 2.23 us -> none  [fused(): pl.pallas_call(functools.partial(block_kernel, nl, nj), out_shape=jax.Sha...]
    pallas_call x1, Pallas kernels: 60.9 us -> 62.3 us  [fused(): pl.pallas_call(functools.partial(block_kernel, nl, nj, rows), out_shape=j...]
    broadcast_in_dim x1 -> x0, local copies, waits for them, and re-layouts: 1.27 us -> none  [fused(): norm_gain[None, :]]
where the time goes in v2:
time: 64.4 us; the launch traced here: 64.2 us
  Pallas kernels  62.3 us (97%)
  local copies, waits for them, and re-layouts  1.91 us (3%)
    pallas_call x1, Pallas kernels, fused(): pl.pallas_call(functools.partial(block_kernel, nl, nj, rows), out_shape=j...  62.3 us
    unnamed x1, local copies, waits for them, and re-layouts  1.91 us

profile of v2, /device:TPU:19, one launch (start us, length us, event | category | flops | bytes accessed | tf_op | source)
XLA Modules:
  0.0 64.2 jit_solution(14728749735951993068)
XLA Ops:
  0.0 62.3 %block.1 = f32[224,640]{1,0:T(8,128)} custom-call(f32[224,640]{1,0:T(8,128)} %bitcast.7, f32[25,640]{1,0:T(8,128)} %taps1.1, f32[25,640]{1,0:T(8,128)} %taps2.1, f32[48,160]{1,0:T(8,128)} %gains.1, f32[640]{0:T(1024)} %norm_gain.1, bf16[2,192,224]{2,1,0:T(8,128)(2,1)} %constant.10.clone.fwd, bf16[2,256,192]{2,1,0:T(8,128)(2,1)} %constant.11.clone.back, ...), custom_call_target="tpu_custom_call" | custom-call | tf_op jit(solution)/shard_map/block/pallas_call | solution.py:589
  62.3 1.9 %copy.14 = f32[8,28,640]{2,0,1:T(8,128)} copy(f32[8,28,640]{2,0,1:T(8,128)} %bitcast.6) | data formatting | bytes 1146880

commit v3 on v2

--- a/solution.py
+++ b/solution.py
@@ -420,14 +420,14 @@
     def c_copy(t, a, b, source):
         return rcopy(
             sent_c.at[a, nj * t + b], spec_in.at[t, span(source * TILE, TILE), :],
-            c_s.at[t, a * nj + b], c_r.at[t, source], a, b,
+            c_s.at[t], c_r.at[t], a, b,
         )
 
     def b_copy(t, a, b, la, lo):
         peer = a * nj + b
         return rcopy(
             spec_out.at[t, span(peer * TILE, TILE), :], got_c.at[la, nj * t + lo],
-            b_s.at[t, peer], b_r.at[t, la * nj + lo], a, b,
+            b_s.at[t], b_r.at[t], a, b,
         )
 
     def keep_c(t):
@@ -436,10 +436,22 @@
     def others(action):
         def step(d, carry):
             peer = lax.rem(me + d, total)
-            action(peer, peer // nj, lax.rem(peer, nj))
+            action(peer, lax.div(peer, nj), lax.rem(peer, nj))
             return carry
 
         lax.fori_loop(1, total, step, 0)
+
+    def tiles(t, count, send, recv):
+        block = spec_in.at[t, pl.ds(0, count * TILE), :]
+        return rcopy(block, block, send.at[t], recv.at[t], below, right)
+
+    def partners(t, action):
+        owners = min(nj, units - nj * t)
+        if owners == nj:
+            action(total - 1)
+        else:
+            pl.when(lo < owners)(lambda: action(nl * owners - 1))
+            pl.when(lo >= owners)(lambda: action(nl * owners))
 
     def own_unit(t, action):
         if nj * t + nj <= units:
@@ -481,7 +493,7 @@
     loads[1].wait()
 
     def filter_unit(t):
-        others(lambda peer, a, b: c_copy(t, la, lo, peer).wait_recv())
+        tiles(t, total - 1, c_s, c_r).wait_recv()
         unit = nj * t + lo
         block = unit // groups
         group = lax.rem(unit, groups)
@@ -509,7 +521,7 @@
             t = unit // nj
             if t not in taken:
                 taken.add(t)
-                others(lambda peer, a, b, t=t: real_unit(t, b, b_copy(t, la, lo, a, b).wait_recv))
+                partners(t, lambda count, t=t: tiles(t, count, b_s, b_r).wait_recv())
         coeffs = got_c[:, block * groups : (block + 1) * groups].reshape(nl * groups * TILE, LANES)
         values = circle[:, :, lanes(block)].reshape(nj * part, LANES)
         high, low = halves(values)
@@ -568,8 +580,8 @@
             guarded(send, copy.wait_send)
 
     for t in range(per):
-        others(lambda peer, a, b, t=t: real_unit(t, b, c_copy(t, a, b, me).wait_send))
-        own_unit(t, lambda t=t: others(lambda peer, a, b: b_copy(t, a, b, la, lo).wait_send()))
+        partners(t, lambda count, t=t: tiles(t, count, c_s, c_r).wait_send())
+        own_unit(t, lambda t=t: tiles(t, total - 1, b_s, b_r).wait_send())
 
 
 def fused(nl, nj, latent, conv_first, conv_second, filter_gains, norm_gain, up_weight, down_weight):
@@ -617,7 +629,7 @@
             vm(*pt.shape[1:], kind=bf16),
             dma(4), dma(blocks), dma(blocks),
             dma(2), dma(2), dma(2, 3), dma(2, 3), dma(nj), dma(nj),
-            dma(blocks, nj), dma(blocks, nj), dma(per, total), dma(per, total), dma(per, total), dma(per, total),
+            dma(blocks, nj), dma(blocks, nj), dma(per), dma(per), dma(per), dma(per),
             dma(blocks, nj), dma(blocks, nj), dma(blocks, 2), dma(blocks, 2),
         ],
         compiler_params=pltpu.CompilerParams(

time: 64.4 us -> 55.5 us (0.86)
  Pallas kernels: 62.3 us -> 53.4 us
    pallas_call x1, Pallas kernels: 62.3 us -> 53.4 us  [fused(): pl.pallas_call(functools.partial(block_kernel, nl, nj, rows), out_shape=j...]
where the time goes in v3:
time: 55.5 us; the launch traced here: 55.3 us
  Pallas kernels  53.4 us (96%)
  local copies, waits for them, and re-layouts  1.91 us (3%)
    pallas_call x1, Pallas kernels, fused(): pl.pallas_call(functools.partial(block_kernel, nl, nj, rows), out_shape=j...  53.4 us
    unnamed x1, local copies, waits for them, and re-layouts  1.91 us

profile of v3, /device:TPU:19, one launch (start us, length us, event | category | flops | bytes accessed | tf_op | source)
XLA Modules:
  0.0 55.3 jit_solution(5168714357242161539)
XLA Ops:
  0.0 53.4 %block.1 = f32[224,640]{1,0:T(8,128)} custom-call(f32[224,640]{1,0:T(8,128)} %bitcast.7, f32[25,640]{1,0:T(8,128)} %taps1.1, f32[25,640]{1,0:T(8,128)} %taps2.1, f32[48,160]{1,0:T(8,128)} %gains.1, f32[640]{0:T(1024)} %norm_gain.1, bf16[2,192,224]{2,1,0:T(8,128)(2,1)} %constant.10.clone.fwd, bf16[2,256,192]{2,1,0:T(8,128)(2,1)} %constant.11.clone.back, ...), custom_call_target="tpu_custom_call" | custom-call | tf_op jit(solution)/shard_map/block/pallas_call | solution.py:601
  53.4 1.9 %copy.14 = f32[8,28,640]{2,0,1:T(8,128)} copy(f32[8,28,640]{2,0,1:T(8,128)} %bitcast.6) | data formatting | bytes 1146880

commit v4 on v3

--- a/solution.py
+++ b/solution.py
@@ -329,15 +329,20 @@
 
     barrier = pltpu.get_barrier_semaphore()
 
-    def greet(d, carry):
-        peer = lax.rem(me + d, total)
+    def greet(a, b):
         pl.semaphore_signal(
-            barrier, inc=1, device_id={"lat": peer // nj, "lon": lax.rem(peer, nj)},
-            device_id_type=pl.DeviceIdType.MESH,
-        )
+            barrier, inc=1, device_id={"lat": a, "lon": b}, device_id_type=pl.DeviceIdType.MESH
+        )
+
+    def greet_band(d, carry):
+        a = lax.rem(la + d, nl)
+        for b in range(nj):
+            greet(a, b)
         return carry
 
-    lax.fori_loop(1, total, greet, 0)
+    for d in range(1, nj):
+        greet(la, lax.rem(lo + d, nj))
+    lax.fori_loop(1, nl, greet_band, 0)
     for block in range(blocks):
         in_copy(block).wait()
         for i in range(rows):
@@ -434,12 +439,17 @@
         spec_in[t, span(me * TILE, TILE), :] = sent_c[la, nj * t + lo]
 
     def others(action):
+        for d in range(1, nj):
+            b = lax.rem(lo + d, nj)
+            action(la * nj + b, la, b)
+
         def step(d, carry):
-            peer = lax.rem(me + d, total)
-            action(peer, lax.div(peer, nj), lax.rem(peer, nj))
+            a = lax.rem(la + d, nl)
+            for b in range(nj):
+                action(a * nj + b, a, b)
             return carry
 
-        lax.fori_loop(1, total, step, 0)
+        lax.fori_loop(1, nl, step, 0)
 
     def tiles(t, count, send, recv):
         block = spec_in.at[t, pl.ds(0, count * TILE), :]
@@ -462,6 +472,9 @@
     def real_unit(t, b, action):
         if nj * t + nj <= units:
             action()
+        elif isinstance(b, int):
+            if nj * t + b < units:
+                action()
         else:
             pl.when(nj * t + b < units)(action)
 

time: 55.5 us -> 55.5 us (level)
  no operation moved by 1% of the time
where the time goes in v4:
time: 55.5 us; the launch traced here: 55.3 us
  Pallas kernels  53.4 us (96%)
  local copies, waits for them, and re-layouts  1.91 us (3%)
    pallas_call x1, Pallas kernels, fused(): pl.pallas_call(functools.partial(block_kernel, nl, nj, rows), out_shape=j...  53.4 us
    unnamed x1, local copies, waits for them, and re-layouts  1.91 us

profile of v4, /device:TPU:19, one launch (start us, length us, event | category | flops | bytes accessed | tf_op | source)
XLA Modules:
  0.0 55.3 jit_solution(5532122155479237606)
XLA Ops:
  0.0 53.4 %block.1 = f32[224,640]{1,0:T(8,128)} custom-call(f32[224,640]{1,0:T(8,128)} %bitcast.7, f32[25,640]{1,0:T(8,128)} %taps1.1, f32[25,640]{1,0:T(8,128)} %taps2.1, f32[48,160]{1,0:T(8,128)} %gains.1, f32[640]{0:T(1024)} %norm_gain.1, bf16[2,192,224]{2,1,0:T(8,128)(2,1)} %constant.10.clone.fwd, bf16[2,256,192]{2,1,0:T(8,128)(2,1)} %constant.11.clone.back, ...), custom_call_target="tpu_custom_call" | custom-call | tf_op jit(solution)/shard_map/block/pallas_call | solution.py:614
  53.4 1.9 %copy.14 = f32[8,28,640]{2,0,1:T(8,128)} copy(f32[8,28,640]{2,0,1:T(8,128)} %bitcast.6) | data formatting | bytes 1146880
